TPU v7x, 32 devices: a whole 2x2x4 slice. The times are simulated.
32 devices in a mesh: dp: 8 (over z, x), tensor: 4 (over y, core).
Axes of the slice: x: 2, y: 2, z: 4, core: 2. Of those that a mesh axis runs over, the one named last changes fastest.
Arguments:
- tokens: bfloat16 [16, 1024, 2048], P('dp', 'tensor'), may hold values from -6 to 6
- pre_gain: float32 [2048], replicated, may hold values from 0.1 to 1.9
- weight_gate: bfloat16 [2048, 4096], P(None, 'tensor'), may hold values from -0.125 to 0.125
- weight_inner: bfloat16 [2048, 4096], P(None, 'tensor'), may hold values from -0.125 to 0.125
- weight_step: bfloat16 [2048, 64], P(None, 'tensor'), may hold values from -0.0625 to 0.0625
- weight_shared: bfloat16 [2048, 256], replicated, may hold values from -0.125 to 0.125
- conv_kernel: float32 [4, 4096], P(None, 'tensor'), may hold values from -3 to 3
- conv_offset: float32 [4096], P('tensor'), may hold values from -1.8 to 1.8
- shared_kernel: float32 [4, 256], replicated, may hold values from -3 to 3
- shared_offset: float32 [256], replicated, may hold values from -1.8 to 1.8
- step_bias: float32 [64], P('tensor'), may hold values from -7 to -2.3
- log_rate: float32 [64], P('tensor'), may hold values from 0 to 2.77
- skip_gain: float32 [64], P('tensor'), may hold values from 0.5 to 2
- gate_gain: float32 [4096], P('tensor'), may hold values from 0.1 to 1.9
- weight_out: bfloat16 [4096, 2048], P('tensor'), may hold values from -0.09375 to 0.09375
- cotangent: bfloat16 [16, 1024, 2048], P('dp', 'tensor'), may hold values from -6 to 6
- segments: int32 [16, 1024], P('dp'), may hold values from 0 to 7, never falling along the last dimension, each value on 1 to 512 neighbouring positions
- image_span: int32 [16, 2], P('dp'), may hold values from 0 to 4, as said below
Outputs:
- block_out: bfloat16 [16, 1024, 2048], P('dp', 'tensor')
- tokens_grad: bfloat16 [16, 1024, 2048], P('dp', 'tensor')
- pre_gain_grad: float32 [2048], replicated
- weight_gate_grad: float32 [2048, 4096], P(None, 'tensor')
- weight_inner_grad: float32 [2048, 4096], P(None, 'tensor')
- weight_step_grad: float32 [2048, 64], P(None, 'tensor')
- weight_shared_grad: float32 [2048, 256], replicated
- conv_kernel_grad: float32 [4, 4096], P(None, 'tensor')
- conv_offset_grad: float32 [4096], P('tensor')
- shared_kernel_grad: float32 [4, 256], replicated
- shared_offset_grad: float32 [256], replicated
- step_bias_grad: float32 [64], P('tensor')
- log_rate_grad: float32 [64], P('tensor')
- skip_gain_grad: float32 [64], P('tensor')
- gate_gain_grad: float32 [4096], P('tensor')
- weight_out_grad: float32 [4096, 2048], P('tensor')
Inputs may be any that keep to these rules, and one draw needn't show every extreme that they name: `segments`: along a sequence the document ids never fall; a document has 1 to 512 tokens. `image_span`: each row holds (first image piece, number of image pieces); first + number <= 4; a sequence may have no image piece.
All inputs are finite; a program needn't handle non-finite values.
Results may differ from a plain program's by a relative error of at most 0.0087.
Values may be sent and summed in bfloat16 or wider, within the bound.
No kernel may reach another device: no remote copies, remote signals or barrier semaphores. Data moves between devices by JAX's collectives and lax.ppermute only.
A program may use at most 320 MiB of HBM per device.

v0:
```python
from functools import partial
import jax
import jax.numpy as jnp
from jax import lax
from jax.sharding import PartitionSpec as P

STRETCH = 256
EPSILON = 1e-05
HIGHEST = lax.Precision.HIGHEST
CONTRACT_ROWS = (((0,), (0,)), ((), ()))
CONTRACT_COLUMNS = (((1,), (1,)), ((), ()))


def sigmoid_linear(values):
    return values * jax.nn.sigmoid(values)


def causal_conv(signal, kernel, offset):
    length = signal.shape[0]
    tap_count = kernel.shape[0]
    padded = jnp.pad(signal, ((tap_count - 1, 0), (0, 0)))
    summed = offset[None, :] + kernel[0][None, :] * padded[0:length]
    for tap_index in range(1, tap_count):
        summed = summed + kernel[tap_index][None, :] * padded[tap_index : tap_index + length]
    return summed


def piece_flags(span_row, pieces):
    piece_index = jnp.arange(pieces, dtype=jnp.int32)
    inside = (piece_index >= span_row[0]) & (piece_index < span_row[0] + span_row[1])
    return inside.astype(jnp.int32)


def state_scan(inputs_x, step_size, decay_rate, b_matrix, c_matrix, segment, is_image):
    length, head_count, head_width = inputs_x.shape
    pieces = is_image.shape[0]
    block_len = length // pieces
    log_step = (step_size * decay_rate[None, :]).reshape(pieces, block_len, head_count)
    cumulated = jnp.cumsum(jnp.transpose(log_step, (2, 0, 1)), axis=2)
    weighted_x = jnp.transpose(
        (inputs_x * step_size[:, :, None]).reshape(pieces, block_len, head_count, head_width),
        (2, 0, 1, 3),
    )
    b_blocks = b_matrix.reshape(pieces, block_len, -1)
    c_blocks = c_matrix.reshape(pieces, block_len, -1)
    doc_blocks = segment.reshape(pieces, block_len)
    same_doc = doc_blocks[:, :, None] == doc_blocks[:, None, :]
    position = jnp.arange(block_len)
    causal = position[:, None] >= position[None, :]
    allowed = same_doc & (causal[None, :, :] | (is_image[:, None, None] > 0))
    spread = cumulated[:, :, :, None] - cumulated[:, :, None, :]
    decays = jnp.where(allowed[None, :, :, :], jnp.exp(-jnp.abs(spread)), jnp.zeros_like(spread))
    scores = jnp.einsum("ctn,csn->cts", c_blocks, b_blocks, precision=HIGHEST)
    mixing = scores[None, :, :, :] * decays
    within = jnp.einsum("hcts,hcsp->hctp", mixing, weighted_x, precision=HIGHEST)
    last_doc = doc_blocks[:, -1]
    to_end = (doc_blocks == last_doc[:, None]).astype(cumulated.dtype)[None, :, :] * jnp.exp(
        cumulated[:, :, -1:] - cumulated
    )
    fresh_state = jnp.einsum(
        "hcsp,csn->chpn", to_end[:, :, :, None] * weighted_x, b_blocks, precision=HIGHEST
    )
    before_doc = jnp.concatenate([doc_blocks[:1, 0], doc_blocks[:-1, -1]])
    keep_factor = (last_doc == before_doc).astype(cumulated.dtype)[:, None] * jnp.transpose(
        jnp.exp(cumulated[:, :, -1])
    )

    def advance(carry_state, scan_item):
        factor, update = scan_item
        return (factor[:, None, None] * carry_state + update, carry_state)

    start_state = jnp.zeros((head_count, head_width, b_blocks.shape[2]), inputs_x.dtype)
    final_state, entering = lax.scan(advance, start_state, (keep_factor, fresh_state))
    reach_gate = (doc_blocks == before_doc[:, None]).astype(cumulated.dtype)[None, :, :] * jnp.exp(
        cumulated
    )
    carried = (
        jnp.einsum("ctn,chpn->hctp", c_blocks, entering, precision=HIGHEST)
        * reach_gate[:, :, :, None]
    )
    total = jnp.transpose(within + carried, (1, 2, 0, 3))
    return total.reshape(length, head_count, head_width)


def state_mixer(
    segment,
    is_image,
    gate_pre,
    inner_pre,
    step_pre,
    shared_pre,
    conv_kernel,
    conv_offset,
    shared_kernel,
    shared_offset,
    step_bias,
    log_rate,
    skip_gain,
):
    activated = sigmoid_linear(causal_conv(inner_pre, conv_kernel, conv_offset))
    shared = sigmoid_linear(causal_conv(shared_pre, shared_kernel, shared_offset))
    state_width = shared.shape[1] // 2
    head_count = step_bias.shape[0]
    length = inner_pre.shape[0]
    inputs_x = activated.reshape(length, head_count, -1)
    step_size = jax.nn.softplus(step_pre + step_bias[None, :])
    decay_rate = -jnp.exp(log_rate)
    mixed_out = state_scan(
        inputs_x,
        step_size,
        decay_rate,
        shared[:, :state_width],
        shared[:, state_width:],
        segment,
        is_image,
    )
    mixed_out = mixed_out + skip_gain[None, :, None] * inputs_x
    return mixed_out.reshape(length, -1) * sigmoid_linear(gate_pre)


def body(
    tokens,
    pre_gain,
    weight_gate,
    weight_inner,
    weight_step,
    weight_shared,
    conv_kernel,
    conv_offset,
    shared_kernel,
    shared_offset,
    step_bias,
    log_rate,
    skip_gain,
    gate_gain,
    weight_out,
    cotangent,
    segments,
    image_span,
):
    micro_count = tokens.shape[0]
    row_count = tokens.shape[1]
    model_width = tokens.shape[2]
    inner_width = weight_gate.shape[1] * lax.axis_size("tensor")
    pieces = segments.shape[1] // STRETCH
    rank_start = lax.axis_index("tensor") * row_count
    running = [
        jnp.zeros(parameter.shape, jnp.float32)
        for parameter in (
            pre_gain,
            weight_gate,
            weight_inner,
            weight_step,
            weight_shared,
            conv_kernel,
            conv_offset,
            shared_kernel,
            shared_offset,
            step_bias,
            log_rate,
            skip_gain,
            gate_gain,
            weight_out,
        )
    ]
    outputs = []
    input_grads = []
    for micro_index in range(micro_count):
        own_rows = tokens[micro_index].astype(jnp.float32)
        row_scale = lax.rsqrt(jnp.mean(own_rows * own_rows, axis=1, keepdims=True) + EPSILON)
        normed_rows = (own_rows * row_scale * pre_gain[None, :]).astype(jnp.bfloat16)
        normed_in = lax.all_gather(normed_rows, "tensor", axis=0, tiled=True)
        gate_pre = jnp.dot(normed_in, weight_gate, preferred_element_type=jnp.float32)
        inner_pre = jnp.dot(normed_in, weight_inner, preferred_element_type=jnp.float32)
        step_pre = jnp.dot(normed_in, weight_step, preferred_element_type=jnp.float32)
        shared_pre = jnp.dot(normed_in, weight_shared, preferred_element_type=jnp.float32)
        is_image = piece_flags(image_span[micro_index], pieces)
        gated_out, mixer_pullback = jax.vjp(
            partial(state_mixer, segments[micro_index], is_image),
            gate_pre,
            inner_pre,
            step_pre,
            shared_pre,
            conv_kernel,
            conv_offset,
            shared_kernel,
            shared_offset,
            step_bias,
            log_rate,
            skip_gain,
        )
        square_sum = lax.psum(jnp.sum(gated_out * gated_out, axis=1), "tensor")
        gate_scale = lax.rsqrt(square_sum / inner_width + EPSILON)[:, None]
        normed_out = (gated_out * gate_scale * gate_gain[None, :]).astype(jnp.bfloat16)
        mixed_rows = lax.psum_scatter(
            jnp.dot(normed_out, weight_out, preferred_element_type=jnp.float32),
            "tensor",
            scatter_dimension=0,
            tiled=True,
        )
        outputs.append((own_rows + mixed_rows).astype(jnp.bfloat16))
        cot_rows = cotangent[micro_index]
        cot_full = lax.all_gather(cot_rows, "tensor", axis=0, tiled=True)
        normed_grad = lax.dot_general(
            cot_full, weight_out, CONTRACT_COLUMNS, preferred_element_type=jnp.float32
        )
        running[13] = running[13] + lax.dot_general(
            normed_out, cot_full, CONTRACT_ROWS, preferred_element_type=jnp.float32
        )
        running[12] = running[12] + jnp.sum(normed_grad * gated_out * gate_scale, axis=0)
        scaled_grad = normed_grad * gate_gain[None, :]
        coupling = lax.psum(jnp.sum(scaled_grad * gated_out, axis=1), "tensor")
        cubed_scale = gate_scale * gate_scale * gate_scale
        gated_grad = (
            gate_scale * scaled_grad - cubed_scale / inner_width * gated_out * coupling[:, None]
        )
        pieces_grad = mixer_pullback(gated_grad)
        for slot_index in range(4, 11):
            running[slot_index + 1] = running[slot_index + 1] + pieces_grad[slot_index]
        shared_full = lax.psum(pieces_grad[3], "tensor")
        gate_low = pieces_grad[0].astype(jnp.bfloat16)
        inner_low = pieces_grad[1].astype(jnp.bfloat16)
        step_low = pieces_grad[2].astype(jnp.bfloat16)
        shared_low = shared_full.astype(jnp.bfloat16)
        running[1] = running[1] + lax.dot_general(
            normed_in, gate_low, CONTRACT_ROWS, preferred_element_type=jnp.float32
        )
        running[2] = running[2] + lax.dot_general(
            normed_in, inner_low, CONTRACT_ROWS, preferred_element_type=jnp.float32
        )
        running[3] = running[3] + lax.dot_general(
            normed_in, step_low, CONTRACT_ROWS, preferred_element_type=jnp.float32
        )
        running[4] = running[4] + lax.dot_general(
            normed_in, shared_low, CONTRACT_ROWS, preferred_element_type=jnp.float32
        )
        summed = lax.dot_general(
            gate_low, weight_gate, CONTRACT_COLUMNS, preferred_element_type=jnp.float32
        )
        summed = summed + lax.dot_general(
            inner_low, weight_inner, CONTRACT_COLUMNS, preferred_element_type=jnp.float32
        )
        input_part = lax.psum_scatter(
            summed
            + lax.dot_general(
                step_low, weight_step, CONTRACT_COLUMNS, preferred_element_type=jnp.float32
            ),
            "tensor",
            scatter_dimension=0,
            tiled=True,
        )
        shared_rows = lax.dynamic_slice_in_dim(shared_low, rank_start, row_count, 0)
        normed_in_grad = input_part + lax.dot_general(
            shared_rows, weight_shared, CONTRACT_COLUMNS, preferred_element_type=jnp.float32
        )
        weighted_grad = normed_in_grad * pre_gain[None, :]
        projection = jnp.sum(weighted_grad * own_rows, axis=1, keepdims=True)
        cubed_row = row_scale * row_scale * row_scale
        own_grad = row_scale * weighted_grad - cubed_row / model_width * own_rows * projection
        running[0] = running[0] + jnp.sum(normed_in_grad * own_rows * row_scale, axis=0)
        input_grads.append((cot_rows.astype(jnp.float32) + own_grad).astype(jnp.bfloat16))
    reduced = lax.psum(
        (
            running[1],
            running[2],
            running[3],
            running[4],
            running[5],
            running[6],
            running[9],
            running[10],
            running[11],
            running[12],
            running[13],
        ),
        "dp",
    )
    (
        grad_gate,
        grad_inner,
        grad_step,
        grad_shared,
        grad_kernel,
        grad_offset,
        grad_bias,
        grad_rate,
        grad_skip,
        grad_gain,
        grad_out,
    ) = reduced
    shared_sums = lax.psum((running[0], running[7], running[8]), ("dp", "tensor"))
    return (
        jnp.stack(outputs),
        jnp.stack(input_grads),
        shared_sums[0],
        grad_gate,
        grad_inner,
        grad_step,
        grad_shared,
        grad_kernel,
        grad_offset,
        shared_sums[1],
        shared_sums[2],
        grad_bias,
        grad_rate,
        grad_skip,
        grad_gain,
        grad_out,
    )


def solution(mesh):
    placed = (
        P("dp", "tensor", None),
        P(),
        P(None, "tensor"),
        P(None, "tensor"),
        P(None, "tensor"),
        P(),
        P(None, "tensor"),
        P("tensor"),
        P(),
        P(),
        P("tensor"),
        P("tensor"),
        P("tensor"),
        P("tensor"),
        P("tensor", None),
        P("dp", "tensor", None),
        P("dp", None),
        P("dp", None),
    )
    return jax.shard_map(
        body,
        mesh=mesh,
        in_specs=placed,
        out_specs=(
            P("dp", "tensor", None),
            P("dp", "tensor", None),
            P(),
            P(None, "tensor"),
            P(None, "tensor"),
            P(None, "tensor"),
            P(),
            P(None, "tensor"),
            P("tensor"),
            P(),
            P(),
            P("tensor"),
            P("tensor"),
            P("tensor"),
            P("tensor"),
            P("tensor", None),
        ),
        check_vma=False,
    )
```

profile of v0, /device:TPU:0, one launch (start us, length us, event | category | flops | bytes accessed | tf_op | source)
XLA Modules:
  0.0 1913.7 jit_solution(8220009131876546524)
XLA Ops:
  28.7 22.6 %all-gather.9.cloned.1.call-done = bf16[1024,2048]{1,0:T(8,128)(2,1)} async-done(((bf16[256,2048]{1,0:T(8,128)(2,1)}), bf16[1024,2048]{1,0:T(8,128)(2,1)}) %all-gather.9.cloned.1.call-update) | async-done | bytes 4194320 | tf_op jit(solution)/shard_map/all_gather | solution.py:172
  58.2 29.8 %all-gather.7.cloned.1.call-done = bf16[1024,2048]{1,0:T(8,128)(2,1)} async-done(((bf16[256,2048]{1,0:T(8,128)(2,1)}), bf16[1024,2048]{1,0:T(8,128)(2,1)}) %all-gather.7.cloned.1.call-update) | async-done | bytes 4194320 | tf_op jit(solution)/shard_map/all_gather | solution.py:172
  121.1 19.4 %fusion.71 = (f32[1024,1024]{1,0:T(8,128)}, f32[1024,1024]{1,0:T(8,128)}, f32[1024,1024]{1,0:T(8,128)}, f32[1024,1024]{1,0:T(8,128)}) fusion(f32[1024,1024]{1,0:T(8,128)} %fusion.234, f32[1024]{0:T(1024)S(1)} %bitcast.580, f32[1024]{0:T(1024)S(1)} %bitcast.582, f32[1024]{0:T(1024)S(1)} %bitcast.578, f32[1024]{0:T(1024)S(1)} %bitcast.576, ...), kind=kLoop, calls=%fused_computation.158 | loop fusion | flops 25165824 | bytes 25186304 | tf_op jit(solution)/shard_map/jvp()/mul | solution.py:15
  180.1 17.4 copy.550
  225.7 22.0 %fusion.67 = f32[4,256,16,64]{1,3,0,2:T(8,128)} fusion(f32[4,16,64,256]{3,2,1,0:T(8,128)S(1)} %fusion.235, f32[4,256,16]{1,0,2:T(4,128)S(1)} %copy-done.112, f32[16,4,256]{2,1,0:T(4,128)S(1)} %copy.533, f32[4,256,256]{2,1,0:T(8,128)S(1)} %fusion.233, pred[4,256,256]{2,1,0:T(8,128)(4,1)S(1)} %copy-done.99, f32[4,256,16,64]{1,3,2,0:T(8,128)S(1)} %copy-done.5, ...), kind=kOutput, calls=%fused_computation.123 | convolution fusion | flops 3245342720 | bytes 14090240 | tf_op jit(solution)/shard_map/jvp(hcts,hcsp->hctp)/dot_general | solution.py:55
  247.8 21.6 %fusion.66 = f32[4,256,16,64]{1,3,0,2:T(8,128)} fusion(f32[4,16,64,256]{3,2,1,0:T(8,128)S(1)} %fusion.239, f32[4,256,16]{1,0,2:T(4,128)S(1)} %copy-done.111, f32[16,4,256]{2,1,0:T(4,128)S(1)} %copy.546, f32[4,256,256]{2,1,0:T(8,128)S(1)} %fusion.237, pred[4,256,256]{2,1,0:T(8,128)(4,1)S(1)} %copy-done.97, f32[4,256,16,64]{1,3,2,0:T(8,128)S(1)} %copy-done.7, ...), kind=kOutput, calls=%fused_computation.121 | convolution fusion | flops 3245342720 | bytes 14090240 | tf_op jit(solution)/shard_map/jvp(hcts,hcsp->hctp)/dot_general | solution.py:55
  311.7 10.1 fusion.240
  321.8 16.5 multiply_reduce_fusion.17
  344.4 9.9 fusion.54
  354.4 13.7 multiply_reduce_fusion.1
  373.9 20.4 %multiply_reduce_fusion.2 = (f32[1024]{0:T(1024)}, f32[1024,1024]{1,0:T(8,128)}, bf16[1024,1024]{1,0:T(8,128)(2,1)}, bf16[1024,1024]{1,0:T(8,128)(2,1)}, f32[1024]{0:T(1024)}, /*index=5*/f32[1024,1024]{1,0:T(8,128)}) fusion(f32[1024,1024]{1,0:T(8,128)} %get-tuple-element.659, f32[1024,1024]{1,0:T(8,128)} %fusion.240, f32[1024]{0:T(1024)S(1)} %get-tuple-element.580, ...), kind=kLoop, calls=%fused_computation.126 | loop fusion | flops 54523904 | bytes 54566912 | tf_op jit(solution)/shard_map/transpose(jvp())/reduce_sum | solution.py:117
  411.3 32.3 %fusion.170 = (f32[16,4,256]{2,1,0:T(4,128)}, f32[16,4,256]{2,1,0:T(4,128)}, f32[4,256,256]{2,1,0:T(8,128)}, f32[16,4,256,256]{3,2,1,0:T(8,128)}) fusion(f32[4,256,256]{2,1,0:T(8,128)S(1)} %copy-done.82, pred[4,256,256]{2,1,0:T(8,128)(4,1)S(1)} %copy-done.99, f32[16,4,256]{2,1,0:T(4,128)S(1)} %copy.533, f32[4,256,16,64]{1,0,3,2:T(4,128)S(1)} %copy-done.3, ...), kind=kOutput, calls=%fused_computation.301 | convolution fusion | flops 3297476608 | bytes 27787264 | tf_op jit(solution)/shard_map/transpose(jvp(hcts,hcsp->hctp))/dot_general | solution.py:55
  460.6 32.7 %fusion.172 = (f32[16,4,256]{2,1,0:T(4,128)S(1)}, f32[16,4,256]{2,1,0:T(4,128)S(1)}, f32[4,256,256]{2,1,0:T(8,128)}, f32[16,4,256,256]{3,2,1,0:T(8,128)}) fusion(f32[4,256,256]{2,1,0:T(8,128)S(1)} %copy-done.80, pred[4,256,256]{2,1,0:T(8,128)(4,1)S(1)} %copy-done.98, f32[16,4,256]{2,1,0:T(4,128)S(1)} %copy-done.110, f32[4,256,16,64]{1,0,3,2:T(4,128)S(1)} %copy-done.1, ...), kind=kOutput, calls=%fused_computation.303 | convolution fusion | flops 3297476608 | bytes 27787264 | tf_op jit(solution)/shard_map/transpose(jvp(hcts,hcsp->hctp))/dot_general | solution.py:55
  518.4 11.9 while.71
  549.0 12.0 while.70
  570.2 10.8 fusion.243
  581.1 9.9 reduce-window.34
  591.3 18.0 bitcast_add_fusion.5
  630.0 9.9 reduce-window.36
  640.1 17.9 bitcast_add_fusion.4
  678.5 24.3 %multiply_reduce_fusion.11 = (f32[1024]{0:T(1024)}, f32[1024]{0:T(1024)}, f32[1024]{0:T(1024)}, f32[1024]{0:T(1024)}, f32[1024]{0:T(1024)}, /*index=5*/f32[1024,...) fusion(f32[1024,1024]{1,0:T(8,128)} %fusion.234, ...), kind=kLoop, calls=%fused_computation.135 | loop fusion | flops 44029952 | bytes 50376704 | tf_op jit(solution)/shard_map/transpose(jvp())/reduce_sum | solution.py:24
  702.9 10.5 broadcast_multiply_fusion
  762.6 11.8 fusion.208
  775.0 11.5 fusion.209
  787.4 9.8 fusion.151
  833.7 76.4 %all-reduce.54 = (bf16[1024,256]{1,0:T(8,128)(2,1)}, bf16[1024,256]{1,0:T(8,128)(2,1)}) all-reduce(f32[1024,256]{1,0:T(8,128)S(1)} %pad_add_fusion.6, f32[1024,256]{1,0:T(8,128)S(1)} %pad_add_fusion.9), channel_id=1, replica_groups=mesh['dp'=8,'tensor'=4] {'tensor'}, use_global_device_ids=true, to_apply=%region_48.50 | all-reduce | flops 524288 | bytes 3145728 | tf_op jit(solution)/shard_map/psum | solution.py:220
  936.7 9.6 convolution_add_fusion.1
  946.3 9.2 convolution_add_fusion
  964.2 37.8 %all-reduce.45 = (f32[4,1024]{1,0:T(4,128)}, f32[1024]{0:T(1024)}, f32[16]{0:T(128)}, f32[16]{0:T(128)}, f32[16]{0:T(128)}, /*index=5*/f32[1024]{0:T(1024)}) all-reduce(f32[4,1024]{1,0:T(4,128)S(1)} %add_add_fusion.2, f32[1024]{0:T(1024)S(1)} %add.459, f32[16]{0:T(128)S(1)} %add.462, ...), channel_id=1, replica_groups=mesh['dp'=8,'tensor'=4] {'dp'}, use_global_device_ids=true, to_apply=%region_65.67 | all-reduce | flops 6192 | bytes 49536 | tf_op jit(solution)/shard_map/psum | solution.py:262
  1011.6 37.5 %all-reduce.44 = (f32[2048]{0:T(1024)}, f32[4,256]{1,0:T(4,128)}, f32[256]{0:T(256)}) all-reduce(f32[2048]{0:T(1024)S(1)} %add.453, f32[4,256]{1,0:T(4,128)S(1)} %add_add_fusion.3, f32[256]{0:T(256)S(1)} %add.461), channel_id=1, replica_groups=mesh['dp'=8,'tensor'=4] {'dp','tensor'}, use_global_device_ids=true, to_apply=%region_52.54 | all-reduce | flops 3328 | bytes 26624 | tf_op jit(solution)/shard_map/psum | solution.py:291
  1049.1 20.9 %reduce-scatter.7.cloned.1.call-done = f32[256,2048]{1,0:T(8,128)} async-done(((f32[1024,2048]{1,0:T(8,128)}), f32[256,2048]{1,0:T(8,128)}) %reduce-scatter.7.cloned.1.call-update) | async-done | bytes 2097168 | tf_op jit(solution)/shard_map/reduce_scatter | solution.py:195
  1078.0 810.2 %all-reduce.53.cloned.1.call-done = (f32[2048,1024]{1,0:T(8,128)}, f32[2048,1024]{1,0:T(8,128)}, f32[2048,16]{0,1:T(8,128)}, f32[2048,256]{1,0:T(8,128)}, f32[1024,2048]{1,0:T(8,128)}) async-done(((f32[2048,1024]{1,0:T(8,128)}, f32[2048,1024]{1,0:T(8,128)}, f32[2048,16]{0,1:T(8,128)}, f32[2048,256]{1,0:T(8,128)}, f32[1024,2048]{1,0:T(8,128)}), (f32[2048,1024]{1,0:T(8,128)}, f32[2048,1024]{1,0:T(8,128)}, ...) | async-done | bytes 27394064 | tf_op jit(solution)/shard_map/psum | solution.py:262
  (665 shorter events, 505.3 us)
Async XLA Ops:
  7.2 91.8 %copy-start = (bf16[2048,256]{1,0:T(8,128)(2,1)S(1)}, bf16[2048,256]{1,0:T(8,128)(2,1)}, u32[]{:S(2)}) copy-start(bf16[2048,256]{1,0:T(8,128)(2,1)} %param.32) | copy-start | bytes 3145732
  7.2 44.2 %all-gather.9.cloned.1.call-start = ((), (), s32[]{:S(2)}) async-start(), calls=%async_computation.6 | async-start | bytes 5242880 | tf_op jit(solution)/shard_map/all_gather | solution.py:172
  14.1 74.0 %all-gather.7.cloned.1.call-start = ((), (), s32[]{:S(2)}) async-start(), calls=%async_computation.4 | async-start | bytes 5242880 | tf_op jit(solution)/shard_map/all_gather | solution.py:172
  14.8 329.6 %all-gather.13.cloned.1.call-start = ((), (), s32[]{:S(2)}) async-start(), calls=%async_computation.11 | async-start | bytes 5242880 | tf_op jit(solution)/shard_map/all_gather | solution.py:203
  16.4 338.0 %all-gather.11.cloned.1.call-start = ((), (), s32[]{:S(2)}) async-start(), calls=%async_computation.10 | async-start | bytes 5242880 | tf_op jit(solution)/shard_map/all_gather | solution.py:203
  17.0 985.1 %reduce-scatter.11.cloned.1.call-start = ((), (), s32[]{:S(2)}) async-start(), calls=%async_computation.9 | async-start | bytes 10485760 | tf_op jit(solution)/shard_map/reduce_scatter | solution.py:243
  18.8 73.2 %copy-start.150 = (f32[16]{0:T(128)}, f32[16]{0:T(128)S(1)}, u32[]{:S(2)}) copy-start(f32[16]{0:T(128)S(1)} %exponential_negate_fusion) | copy-start | bytes 196
  19.4 84.4 %copy-start.152 = (f32[1,256]{1,0:T(1,128)}, f32[1,256]{1,0:T(1,128)S(1)}, u32[]{:S(2)}) copy-start(f32[1,256]{1,0:T(1,128)S(1)} %get-tuple-element.699) | copy-start | bytes 3076
  19.4 84.4 %copy-start.154 = (f32[1,256]{1,0:T(1,128)}, f32[1,256]{1,0:T(1,128)S(1)}, u32[]{:S(2)}) copy-start(f32[1,256]{1,0:T(1,128)S(1)} %get-tuple-element.700) | copy-start | bytes 3076
  19.5 84.4 %copy-start.156 = (f32[1,256]{1,0:T(1,128)}, f32[1,256]{1,0:T(1,128)S(1)}, u32[]{:S(2)}) copy-start(f32[1,256]{1,0:T(1,128)S(1)} %get-tuple-element.701) | copy-start | bytes 3076
  19.5 84.4 %copy-start.158 = (f32[1,256]{1,0:T(1,128)}, f32[1,256]{1,0:T(1,128)S(1)}, u32[]{:S(2)}) copy-start(f32[1,256]{1,0:T(1,128)S(1)} %get-tuple-element.702) | copy-start | bytes 3076
  19.6 354.2 %copy-start.119 = (f32[1024]{0:T(1024)}, f32[1024]{0:T(1024)S(1)}, u32[]{:S(2)}) copy-start(f32[1024]{0:T(1024)S(1)} %mul.1247) | copy-start | bytes 12292
  20.2 100.9 %copy-start.121 = (f32[1,1024]{1,0:T(1,128)}, f32[1,1024]{1,0:T(1,128)S(1)}, u32[]{:S(2)}) copy-start(f32[1,1024]{1,0:T(1,128)S(1)} %get-tuple-element.664) | copy-start | bytes 12292
  20.2 100.9 %copy-start.123 = (f32[1,1024]{1,0:T(1,128)}, f32[1,1024]{1,0:T(1,128)S(1)}, u32[]{:S(2)}) copy-start(f32[1,1024]{1,0:T(1,128)S(1)} %get-tuple-element.665) | copy-start | bytes 12292
  20.2 100.9 %copy-start.125 = (f32[1,1024]{1,0:T(1,128)}, f32[1,1024]{1,0:T(1,128)S(1)}, u32[]{:S(2)}) copy-start(f32[1,1024]{1,0:T(1,128)S(1)} %get-tuple-element.666) | copy-start | bytes 12292
  25.0 69.9 %copy-start.168 = (f32[4]{0:T(128)}, f32[4]{0:T(128)S(1)}, u32[]{:S(2)}) copy-start(f32[4]{0:T(128)S(1)} %convert_reduce_fusion) | copy-start | bytes 52
  26.5 70.4 %copy-start.166 = (f32[4]{0:T(128)}, f32[4]{0:T(128)S(1)}, u32[]{:S(2)}) copy-start(f32[4]{0:T(128)S(1)} %convert_reduce_fusion.1) | copy-start | bytes 52
  27.3 70.3 %copy-start.117 = (f32[4,256]{1,0:T(4,128)}, f32[4,256]{1,0:T(4,128)S(1)}, u32[]{:S(2)}) copy-start(f32[4,256]{1,0:T(4,128)S(1)} %get-tuple-element.692) | copy-start | bytes 12292
  27.4 70.3 %copy-start.131 = (f32[4,256]{1,0:T(4,128)}, f32[4,256]{1,0:T(4,128)S(1)}, u32[]{:S(2)}) copy-start(f32[4,256]{1,0:T(4,128)S(1)} %get-tuple-element.691) | copy-start | bytes 12292
  27.4 68.1 %copy-start.115 = (f32[4,256]{1,0:T(4,128)}, f32[4,256]{1,0:T(4,128)S(1)}, u32[]{:S(2)}) copy-start(f32[4,256]{1,0:T(4,128)S(1)} %get-tuple-element.696) | copy-start | bytes 12292
  27.4 68.1 %copy-start.129 = (f32[4,256]{1,0:T(4,128)}, f32[4,256]{1,0:T(4,128)S(1)}, u32[]{:S(2)}) copy-start(f32[4,256]{1,0:T(4,128)S(1)} %get-tuple-element.695) | copy-start | bytes 12292
  58.2 189.5 %copy-start.109 = (f32[16,4,256]{2,1,0:T(4,128)}, f32[16,4,256]{2,1,0:T(4,128)S(1)}, u32[]{:S(2)}) copy-start(f32[16,4,256]{2,1,0:T(4,128)S(1)} %copy.546) | copy-start | bytes 196612
  94.9 152.8 %copy-start.70 = (f32[2,4,8,256]{3,2,0,1:T(8,128)}, f32[2,4,8,256]{3,2,0,1:T(8,128)S(1)}, u32[]{:S(2)}) copy-start(f32[2,4,8,256]{3,2,0,1:T(8,128)S(1)} %copy.764) | copy-start | bytes 196612
  96.3 101.3 %copy-start.75 = (f32[16,4,256]{2,0,1:T(8,128)}, f32[16,4,256]{2,0,1:T(8,128)S(1)}, u32[]{:S(2)}) copy-start(f32[16,4,256]{2,0,1:T(8,128)S(1)} %get-tuple-element.651) | copy-start | bytes 196612
  96.9 464.2 %copy-start.73 = (f32[2,4,8,256]{3,2,0,1:T(8,128)}, f32[2,4,8,256]{3,2,0,1:T(8,128)S(1)}, u32[]{:S(2)}) copy-start(f32[2,4,8,256]{3,2,0,1:T(8,128)S(1)} %copy.765) | copy-start | bytes 196612
  107.4 107.4 %copy-start.36 = (f32[1024,128]{1,0:T(8,128)}, f32[1024,128]{1,0:T(8,128)S(1)}, u32[]{:S(2)}) copy-start(f32[1024,128]{1,0:T(8,128)S(1)} %get-tuple-element.641) | copy-start | bytes 1572868
  109.1 108.0 %copy-start.33 = (f32[1024,128]{1,0:T(8,128)}, f32[1024,128]{1,0:T(8,128)S(1)}, u32[]{:S(2)}) copy-start(f32[1024,128]{1,0:T(8,128)S(1)} %get-tuple-element.643) | copy-start | bytes 1572868
  739.0 267.1 %reduce-scatter.9.cloned.1.call-start = ((), (), s32[]{:S(2)}) async-start(), calls=%async_computation.8 | async-start | bytes 10485760 | tf_op jit(solution)/shard_map/reduce_scatter | solution.py:243
  761.9 287.2 %reduce-scatter.5.cloned.1.call-start = ((), (), s32[]{:S(2)}) async-start(), calls=%async_computation.5 | async-start | bytes 10485760 | tf_op jit(solution)/shard_map/reduce_scatter | solution.py:195
  774.4 295.6 %reduce-scatter.7.cloned.1.call-start = ((), (), s32[]{:S(2)}) async-start(), calls=%async_computation.7 | async-start | bytes 10485760 | tf_op jit(solution)/shard_map/reduce_scatter | solution.py:195
  786.6 1101.6 %all-reduce.53.cloned.1.call-start = ((), (), s32[]{:S(2)}) async-start(), calls=%async_computation.12 | async-start | bytes 54788096 | tf_op jit(solution)/shard_map/psum | solution.py:262
  1006.1 63.9 %copy-start.172 = (f32[256]{0:T(256)S(1)}, f32[256]{0:T(256)}, u32[]{:S(2)}) copy-start(f32[256]{0:T(256)} %get-tuple-element.724) | copy-start | bytes 3076
  (172 other events, 1829.7 us)
Sparse Core Ops, SparseCore 0:
  14.2 37.1 all-gather.8
  53.5 34.4 all-gather.6
  89.6 34.5 all-gather.12
  125.6 34.5 all-gather.10
  739.1 72.4 reduce-scatter.10
  814.8 104.1 reduce-scatter.8
  921.5 72.5 reduce-scatter.4
  997.5 72.4 reduce-scatter.6
  1075.8 812.2 all-reduce.52
where the time goes:
time: 1930 us; the launch traced here: 1910 us
  waiting for transfers between devices  885 us (46%)
  matrix products  439 us (23%)
  local copies, waits for them, and re-layouts  213 us (11%)
  other arithmetic  193 us (10%)
  blocking collectives  164 us (8%)
  between operations  19.4 us (1%)
    psum x1, waiting for transfers between devices, body(): lax.psum((running[1], running[2], running[3], running[4], running[5], run...  810 us
    dot_general x6, matrix products, state_scan(): jnp.einsum('hcts,hcsp->hctp', mixing, weighted_x, precision=HIGHEST)  145 us
    psum x1, blocking collectives, body(): shared_full = lax.psum(pieces_grad[3], 'tensor')  76.4 us
    all_gather x2, waiting for transfers between devices, body(): normed_in = lax.all_gather(normed_rows, 'tensor', axis=0, tiled=True)  52.4 us
    dot_general x6, matrix products, state_scan(): jnp.einsum('hcsp,csn->chpn', to_end[:, :, :, None] * weighted_x, b_blocks...  49.4 us
    reshape x6, local copies, waits for them, and re-layouts, state_scan(): return total.reshape(length, head_count, head_width)  43 us
    another operation x14, other arithmetic  41.7 us
    reshape x6, local copies, waits for them, and re-layouts, state_scan(): (inputs_x * step_size[:, :, None]).reshape(pieces, block_len, head_count,...  41 us
  transfers between devices with their start and end apart: 9, of which 4 were waited for; matrix products, arithmetic and copies ran while one was open for 23% of the time, Pallas kernels for 0%

commit v1 on v0

--- a/solution.py
+++ b/solution.py
@@ -217,7 +217,9 @@
         pieces_grad = mixer_pullback(gated_grad)
         for slot_index in range(4, 11):
             running[slot_index + 1] = running[slot_index + 1] + pieces_grad[slot_index]
-        shared_full = lax.psum(pieces_grad[3], "tensor")
+        part = pieces_grad[3]
+        parts = lax.all_gather(part, "tensor", axis=0, tiled=False)
+        shared_full = parts.sum(axis=0)
         gate_low = pieces_grad[0].astype(jnp.bfloat16)
         inner_low = pieces_grad[1].astype(jnp.bfloat16)
         step_low = pieces_grad[2].astype(jnp.bfloat16)

time: 1930 us -> 1940 us (level)
  waiting for transfers between devices: 885 us -> 965 us
  blocking collectives: 164 us -> 87.3 us
    reduce_scatter x2, waiting for transfers between devices: 20.9 us -> 101 us  [body(): lax.psum_scatter(jnp.dot(normed_out, weight_out, preferred_element_type=j...]
    psum x1 -> x0, blocking collectives: 76.4 us -> none  [body(): shared_full = lax.psum(pieces_grad[3], 'tensor')]
  transfers between devices with their start and end apart: 9 -> 11, of which waited for: 4 -> 5; matrix products, arithmetic and copies ran while one was open for 23% -> 32% of each run, Pallas kernels for 0% -> 0%
where the time goes in v1:
time: 1940 us; the launch traced here: 1930 us
  waiting for transfers between devices  965 us (50%)
  matrix products  434 us (22%)
  local copies, waits for them, and re-layouts  211 us (11%)
  other arithmetic  210 us (11%)
  blocking collectives  87.3 us (4%)
  between operations  19.5 us (1%)
    psum x1, waiting for transfers between devices, body(): lax.psum((running[1], running[2], running[3], running[4], running[5], run...  810 us
    dot_general x6, matrix products, state_scan(): jnp.einsum('hcts,hcsp->hctp', mixing, weighted_x, precision=HIGHEST)  146 us
    reduce_scatter x2, waiting for transfers between devices, body(): lax.psum_scatter(jnp.dot(normed_out, weight_out, preferred_element_type=j...  101 us
    all_gather x2, waiting for transfers between devices, body(): normed_in = lax.all_gather(normed_rows, 'tensor', axis=0, tiled=True)  52.5 us
    dot_general x6, matrix products, state_scan(): jnp.einsum('hcsp,csn->chpn', to_end[:, :, :, None] * weighted_x, b_blocks...  46.7 us
    reshape x6, local copies, waits for them, and re-layouts, state_scan(): return total.reshape(length, head_count, head_width)  43.4 us
    another operation x14, other arithmetic  42.9 us
    reshape x4, local copies, waits for them, and re-layouts, state_mixer(): inputs_x = activated.reshape(length, head_count, -1)  39.7 us
  transfers between devices with their start and end apart: 11, of which 5 were waited for; matrix products, arithmetic and copies ran while one was open for 32% of the time, Pallas kernels for 0%

profile of v1, /device:TPU:0, one launch (start us, length us, event | category | flops | bytes accessed | tf_op | source)
XLA Modules:
  0.0 1928.3 jit_solution(8218082993572906661)
XLA Ops:
  28.7 22.7 %all-gather.13.cloned.1.call-done = bf16[1024,2048]{1,0:T(8,128)(2,1)} async-done(((bf16[256,2048]{1,0:T(8,128)(2,1)}), bf16[1024,2048]{1,0:T(8,128)(2,1)}) %all-gather.13.cloned.1.call-update) | async-done | bytes 4194320 | tf_op jit(solution)/shard_map/all_gather | solution.py:172
  58.3 29.8 %all-gather.11.cloned.1.call-done = bf16[1024,2048]{1,0:T(8,128)(2,1)} async-done(((bf16[256,2048]{1,0:T(8,128)(2,1)}), bf16[1024,2048]{1,0:T(8,128)(2,1)}) %all-gather.11.cloned.1.call-update) | async-done | bytes 4194320 | tf_op jit(solution)/shard_map/all_gather | solution.py:172
  121.1 19.5 %fusion.71 = (f32[1024,1024]{1,0:T(8,128)}, f32[1024,1024]{1,0:T(8,128)}, f32[1024,1024]{1,0:T(8,128)}, f32[1024,1024]{1,0:T(8,128)}) fusion(f32[1024,1024]{1,0:T(8,128)} %fusion.234, f32[1024]{0:T(1024)S(1)} %bitcast.582, f32[1024]{0:T(1024)S(1)} %bitcast.584, f32[1024]{0:T(1024)S(1)} %bitcast.580, f32[1024]{0:T(1024)S(1)} %bitcast.578, ...), kind=kLoop, calls=%fused_computation.158 | loop fusion | flops 25165824 | bytes 25186304 | tf_op jit(solution)/shard_map/jvp()/mul | solution.py:15
  180.1 17.5 copy.550
  227.5 22.1 %fusion.67 = f32[4,256,16,64]{1,3,0,2:T(8,128)} fusion(f32[4,16,64,256]{3,2,1,0:T(8,128)S(1)} %fusion.235, f32[4,256,16]{1,0,2:T(4,128)S(1)} %copy-done.111, f32[16,4,256]{2,1,0:T(4,128)S(1)} %copy.533, f32[4,256,256]{2,1,0:T(8,128)S(1)} %fusion.233, pred[4,256,256]{2,1,0:T(8,128)(4,1)S(1)} %copy-done.95, f32[4,256,16,64]{1,3,2,0:T(8,128)S(1)} %copy-done.5, ...), kind=kOutput, calls=%fused_computation.123 | convolution fusion | flops 3245342720 | bytes 14090240 | tf_op jit(solution)/shard_map/jvp(hcts,hcsp->hctp)/dot_general | solution.py:55
  249.7 21.6 %fusion.66 = f32[4,256,16,64]{1,3,0,2:T(8,128)} fusion(f32[4,16,64,256]{3,2,1,0:T(8,128)S(1)} %fusion.239, f32[4,256,16]{1,0,2:T(4,128)S(1)} %copy-done.110, f32[16,4,256]{2,1,0:T(4,128)S(1)} %copy.546, f32[4,256,256]{2,1,0:T(8,128)S(1)} %fusion.237, pred[4,256,256]{2,1,0:T(8,128)(4,1)S(1)} %copy-done.93, f32[4,256,16,64]{1,3,2,0:T(8,128)S(1)} %copy-done.7, ...), kind=kOutput, calls=%fused_computation.121 | convolution fusion | flops 3245342720 | bytes 14090240 | tf_op jit(solution)/shard_map/jvp(hcts,hcsp->hctp)/dot_general | solution.py:55
  302.9 10.1 fusion.240
  313.0 17.6 multiply_reduce_fusion.17
  336.8 10.0 fusion.54
  346.7 13.7 multiply_reduce_fusion.1
  366.3 20.2 %multiply_reduce_fusion.2 = (f32[1024]{0:T(1024)}, f32[1024,1024]{1,0:T(8,128)}, bf16[1024,1024]{1,0:T(8,128)(2,1)}, bf16[1024,1024]{1,0:T(8,128)(2,1)}, f32[1024]{0:T(1024)}, /*index=5*/f32[1024,1024]{1,0:T(8,128)}) fusion(f32[1024,1024]{1,0:T(8,128)} %get-tuple-element.657, f32[1024,1024]{1,0:T(8,128)} %fusion.240, f32[1024]{0:T(1024)S(1)} %get-tuple-element.578, ...), kind=kLoop, calls=%fused_computation.126 | loop fusion | flops 54523904 | bytes 54566912 | tf_op jit(solution)/shard_map/transpose(jvp())/reduce_sum | solution.py:117
  397.9 10.6 fusion.157
  425.2 10.0 fusion.158
  440.7 33.5 %fusion.170 = (f32[16,4,256]{2,1,0:T(4,128)}, f32[16,4,256]{2,1,0:T(4,128)}, f32[4,256,256]{2,1,0:T(8,128)S(1)}, f32[16,4,256,256]{3,2,1,0:T(8,128)}) fusion(f32[4,256,256]{2,1,0:T(8,128)S(1)} %copy-done.78, pred[4,256,256]{2,1,0:T(8,128)(4,1)S(1)} %copy-done.96, f32[16,4,256]{2,1,0:T(4,128)S(1)} %copy.533, f32[4,256,16,64]{1,0,3,2:T(4,128)S(1)} %copy-done.4, ...), kind=kOutput, calls=%fused_computation.301 | convolution fusion | flops 3297476608 | bytes 27787264 | tf_op jit(solution)/shard_map/transpose(jvp(hcts,hcsp->hctp))/dot_general | solution.py:55
  474.2 33.6 %fusion.172 = (f32[16,4,256]{2,1,0:T(4,128)}, f32[16,4,256]{2,1,0:T(4,128)}, f32[4,256,256]{2,1,0:T(8,128)}, f32[16,4,256,256]{3,2,1,0:T(8,128)}) fusion(f32[4,256,256]{2,1,0:T(8,128)S(1)} %copy-done.76, pred[4,256,256]{2,1,0:T(8,128)(4,1)S(1)} %copy-done.94, f32[16,4,256]{2,1,0:T(4,128)S(1)} %copy-done.109, f32[4,256,16,64]{1,0,3,2:T(4,128)S(1)} %copy-done.2, ...), kind=kOutput, calls=%fused_computation.303 | convolution fusion | flops 3297476608 | bytes 27787264 | tf_op jit(solution)/shard_map/transpose(jvp(hcts,hcsp->hctp))/dot_general | solution.py:55
  509.4 11.8 while.71
  532.3 12.2 while.70
  607.9 9.9 reduce-window.34
  617.9 17.9 bitcast_add_fusion.5
  657.5 16.8 bitcast_add_fusion.4
  698.0 28.3 %multiply_reduce_fusion.11 = (f32[1024]{0:T(1024)}, f32[1024]{0:T(1024)}, f32[1024]{0:T(1024)}, f32[1024]{0:T(1024)}, f32[1024]{0:T(1024)}, /*index=5*/f32[1024,...) fusion(f32[1024,1024]{1,0:T(8,128)} %fusion.234, ...), kind=kLoop, calls=%fused_computation.135 | loop fusion | flops 44029952 | bytes 50376704 | tf_op jit(solution)/shard_map/transpose(jvp())/reduce_sum | solution.py:24
  731.7 9.9 reduce-window.36
  746.6 11.6 broadcast_multiply_fusion
  758.3 9.6 fusion.44
  810.1 11.9 fusion.208
  822.7 11.5 fusion.209
  867.1 10.5 convolution_add_fusion
  899.5 37.9 %all-reduce.45 = (f32[4,1024]{1,0:T(4,128)}, f32[1024]{0:T(1024)}, f32[16]{0:T(128)}, f32[16]{0:T(128)}, f32[16]{0:T(128)}, /*index=5*/f32[1024]{0:T(1024)}) all-reduce(f32[4,1024]{1,0:T(4,128)S(1)} %add_add_fusion.2, f32[1024]{0:T(1024)S(1)} %add.455, f32[16]{0:T(128)S(1)} %add.458, ...), channel_id=1, replica_groups=mesh['dp'=8,'tensor'=4] {'dp'}, use_global_device_ids=true, to_apply=%region_65.67 | all-reduce | flops 6192 | bytes 49536 | tf_op jit(solution)/shard_map/psum | solution.py:264
  946.2 37.5 %all-reduce.44 = (f32[2048]{0:T(1024)}, f32[4,256]{1,0:T(4,128)}, f32[256]{0:T(256)}) all-reduce(f32[2048]{0:T(1024)S(1)} %add.449, f32[4,256]{1,0:T(4,128)S(1)} %add_add_fusion.3, f32[256]{0:T(256)S(1)} %add.457), channel_id=1, replica_groups=mesh['dp'=8,'tensor'=4] {'dp','tensor'}, use_global_device_ids=true, to_apply=%region_52.54 | all-reduce | flops 3328 | bytes 26624 | tf_op jit(solution)/shard_map/psum | solution.py:293
  983.7 25.9 %reduce-scatter.5.cloned.1.call-done = f32[256,2048]{1,0:T(8,128)} async-done(((f32[1024,2048]{1,0:T(8,128)}), f32[256,2048]{1,0:T(8,128)}) %reduce-scatter.5.cloned.1.call-update) | async-done | bytes 2097168 | tf_op jit(solution)/shard_map/reduce_scatter | solution.py:195
  1009.6 74.9 %reduce-scatter.7.cloned.1.call-done = f32[256,2048]{1,0:T(8,128)} async-done(((f32[1024,2048]{1,0:T(8,128)}), f32[256,2048]{1,0:T(8,128)}) %reduce-scatter.7.cloned.1.call-update) | async-done | bytes 2097168 | tf_op jit(solution)/shard_map/reduce_scatter | solution.py:195
  1092.5 810.4 %all-reduce.51.cloned.1.call-done = (f32[2048,1024]{1,0:T(8,128)}, f32[2048,1024]{1,0:T(8,128)}, f32[2048,16]{0,1:T(8,128)}, f32[2048,256]{1,0:T(8,128)}, f32[1024,2048]{1,0:T(8,128)}) async-done(((f32[2048,1024]{1,0:T(8,128)}, f32[2048,1024]{1,0:T(8,128)}, f32[2048,16]{0,1:T(8,128)}, f32[2048,256]{1,0:T(8,128)}, f32[1024,2048]{1,0:T(8,128)}), (f32[2048,1024]{1,0:T(8,128)}, f32[2048,1024]{1,0:T(8,128)}, ...) | async-done | bytes 27394064 | tf_op jit(solution)/shard_map/psum | solution.py:264
  (690 shorter events, 507.4 us)
Async XLA Ops:
  7.2 91.9 %copy-start = (bf16[2048,256]{1,0:T(8,128)(2,1)S(1)}, bf16[2048,256]{1,0:T(8,128)(2,1)}, u32[]{:S(2)}) copy-start(bf16[2048,256]{1,0:T(8,128)(2,1)} %param.32) | copy-start | bytes 3145732
  7.2 44.2 %all-gather.13.cloned.1.call-start = ((), (), s32[]{:S(2)}) async-start(), calls=%async_computation.6 | async-start | bytes 5242880 | tf_op jit(solution)/shard_map/all_gather | solution.py:172
  14.1 74.0 %all-gather.11.cloned.1.call-start = ((), (), s32[]{:S(2)}) async-start(), calls=%async_computation.4 | async-start | bytes 5242880 | tf_op jit(solution)/shard_map/all_gather | solution.py:172
  14.9 321.9 %all-gather.19.cloned.1.call-start = ((), (), s32[]{:S(2)}) async-start(), calls=%async_computation.12 | async-start | bytes 5242880 | tf_op jit(solution)/shard_map/all_gather | solution.py:203
  16.4 330.4 %all-gather.15.cloned.1.call-start = ((), (), s32[]{:S(2)}) async-start(), calls=%async_computation.10 | async-start | bytes 5242880 | tf_op jit(solution)/shard_map/all_gather | solution.py:203
  17.0 869.2 %all-gather.21.cloned.1.call-start = ((), (), s32[]{:S(2)}) async-start(), calls=%async_computation.13 | async-start | bytes 5242880 | tf_op jit(solution)/shard_map/all_gather | solution.py:221
  18.8 73.3 %copy-start.151 = (f32[16]{0:T(128)}, f32[16]{0:T(128)S(1)}, u32[]{:S(2)}) copy-start(f32[16]{0:T(128)S(1)} %exponential_negate_fusion) | copy-start | bytes 196
  19.4 84.5 %copy-start.153 = (f32[1,256]{1,0:T(1,128)}, f32[1,256]{1,0:T(1,128)S(1)}, u32[]{:S(2)}) copy-start(f32[1,256]{1,0:T(1,128)S(1)} %get-tuple-element.697) | copy-start | bytes 3076
  19.4 84.5 %copy-start.155 = (f32[1,256]{1,0:T(1,128)}, f32[1,256]{1,0:T(1,128)S(1)}, u32[]{:S(2)}) copy-start(f32[1,256]{1,0:T(1,128)S(1)} %get-tuple-element.698) | copy-start | bytes 3076
  19.4 84.5 %copy-start.157 = (f32[1,256]{1,0:T(1,128)}, f32[1,256]{1,0:T(1,128)S(1)}, u32[]{:S(2)}) copy-start(f32[1,256]{1,0:T(1,128)S(1)} %get-tuple-element.699) | copy-start | bytes 3076
  19.4 84.5 %copy-start.159 = (f32[1,256]{1,0:T(1,128)}, f32[1,256]{1,0:T(1,128)S(1)}, u32[]{:S(2)}) copy-start(f32[1,256]{1,0:T(1,128)S(1)} %get-tuple-element.700) | copy-start | bytes 3076
  19.6 346.6 %copy-start.120 = (f32[1024]{0:T(1024)}, f32[1024]{0:T(1024)S(1)}, u32[]{:S(2)}) copy-start(f32[1024]{0:T(1024)S(1)} %mul.1247) | copy-start | bytes 12292
  20.2 100.9 %copy-start.122 = (f32[1,1024]{1,0:T(1,128)}, f32[1,1024]{1,0:T(1,128)S(1)}, u32[]{:S(2)}) copy-start(f32[1,1024]{1,0:T(1,128)S(1)} %get-tuple-element.662) | copy-start | bytes 12292
  20.2 100.9 %copy-start.124 = (f32[1,1024]{1,0:T(1,128)}, f32[1,1024]{1,0:T(1,128)S(1)}, u32[]{:S(2)}) copy-start(f32[1,1024]{1,0:T(1,128)S(1)} %get-tuple-element.663) | copy-start | bytes 12292
  20.2 100.9 %copy-start.126 = (f32[1,1024]{1,0:T(1,128)}, f32[1,1024]{1,0:T(1,128)S(1)}, u32[]{:S(2)}) copy-start(f32[1,1024]{1,0:T(1,128)S(1)} %get-tuple-element.664) | copy-start | bytes 12292
  25.0 70.0 %copy-start.169 = (f32[4]{0:T(128)}, f32[4]{0:T(128)S(1)}, u32[]{:S(2)}) copy-start(f32[4]{0:T(128)S(1)} %convert_reduce_fusion) | copy-start | bytes 52
  26.5 70.5 %copy-start.167 = (f32[4]{0:T(128)}, f32[4]{0:T(128)S(1)}, u32[]{:S(2)}) copy-start(f32[4]{0:T(128)S(1)} %convert_reduce_fusion.1) | copy-start | bytes 52
  27.3 70.3 %copy-start.118 = (f32[4,256]{1,0:T(4,128)}, f32[4,256]{1,0:T(4,128)S(1)}, u32[]{:S(2)}) copy-start(f32[4,256]{1,0:T(4,128)S(1)} %get-tuple-element.690) | copy-start | bytes 12292
  27.3 70.3 %copy-start.132 = (f32[4,256]{1,0:T(4,128)}, f32[4,256]{1,0:T(4,128)S(1)}, u32[]{:S(2)}) copy-start(f32[4,256]{1,0:T(4,128)S(1)} %get-tuple-element.689) | copy-start | bytes 12292
  27.4 68.2 %copy-start.130 = (f32[4,256]{1,0:T(4,128)}, f32[4,256]{1,0:T(4,128)S(1)}, u32[]{:S(2)}) copy-start(f32[4,256]{1,0:T(4,128)S(1)} %get-tuple-element.693) | copy-start | bytes 12292
  58.3 191.4 %copy-start.108 = (f32[16,4,256]{2,1,0:T(4,128)}, f32[16,4,256]{2,1,0:T(4,128)S(1)}, u32[]{:S(2)}) copy-start(f32[16,4,256]{2,1,0:T(4,128)S(1)} %copy.546) | copy-start | bytes 196612
  94.9 154.7 %copy-start.69 = (f32[2,4,8,256]{3,2,0,1:T(8,128)}, f32[2,4,8,256]{3,2,0,1:T(8,128)S(1)}, u32[]{:S(2)}) copy-start(f32[2,4,8,256]{3,2,0,1:T(8,128)S(1)} %copy.764) | copy-start | bytes 196612
  96.3 101.3 %copy-start.71 = (f32[16,4,256]{2,0,1:T(8,128)}, f32[16,4,256]{2,0,1:T(8,128)S(1)}, u32[]{:S(2)}) copy-start(f32[16,4,256]{2,0,1:T(8,128)S(1)} %get-tuple-element.649) | copy-start | bytes 196612
  109.1 88.5 %copy-start.30 = (f32[1024,128]{1,0:T(8,128)}, f32[1024,128]{1,0:T(8,128)S(1)}, u32[]{:S(2)}) copy-start(f32[1024,128]{1,0:T(8,128)S(1)} %get-tuple-element.641) | copy-start | bytes 1572868
  566.6 322.3 %all-gather.17.cloned.1.call-start = ((), (), s32[]{:S(2)}) async-start(), calls=%async_computation.11 | async-start | bytes 5242880 | tf_op jit(solution)/shard_map/all_gather | solution.py:221
  697.9 239.6 %reduce-scatter.11.cloned.1.call-start = ((), (), s32[]{:S(2)}) async-start(), calls=%async_computation.9 | async-start | bytes 10485760 | tf_op jit(solution)/shard_map/reduce_scatter | solution.py:245
  787.1 153.9 %reduce-scatter.9.cloned.1.call-start = ((), (), s32[]{:S(2)}) async-start(), calls=%async_computation.8 | async-start | bytes 10485760 | tf_op jit(solution)/shard_map/reduce_scatter | solution.py:245
  809.4 200.2 %reduce-scatter.5.cloned.1.call-start = ((), (), s32[]{:S(2)}) async-start(), calls=%async_computation.5 | async-start | bytes 10485760 | tf_op jit(solution)/shard_map/reduce_scatter | solution.py:195
  822.0 262.5 %reduce-scatter.7.cloned.1.call-start = ((), (), s32[]{:S(2)}) async-start(), calls=%async_computation.7 | async-start | bytes 10485760 | tf_op jit(solution)/shard_map/reduce_scatter | solution.py:195
  834.2 1068.6 %all-reduce.51.cloned.1.call-start = ((), (), s32[]{:S(2)}) async-start(), calls=%async_computation.14 | async-start | bytes 54788096 | tf_op jit(solution)/shard_map/psum | solution.py:264
  940.9 143.6 %copy-start.172 = (f32[256]{0:T(256)S(1)}, f32[256]{0:T(256)}, u32[]{:S(2)}) copy-start(f32[256]{0:T(256)} %get-tuple-element.701) | copy-start | bytes 3076
  941.0 143.6 %copy-start.173 = (f32[256]{0:T(256)S(1)}, f32[256]{0:T(256)}, u32[]{:S(2)}) copy-start(f32[256]{0:T(256)} %get-tuple-element.722) | copy-start | bytes 3076
  (184 other events, 2276.4 us)
Sparse Core Ops, SparseCore 0:
  14.2 37.1 all-gather.12
  53.6 34.4 all-gather.10
  89.6 34.5 all-gather.18
  125.6 34.5 all-gather.14
  566.7 35.1 all-gather.20
  698.0 35.1 all-gather.16
  787.2 72.1 reduce-scatter.10
  862.7 71.7 reduce-scatter.8
  937.1 72.4 reduce-scatter.4
  1012.8 71.7 reduce-scatter.6
  1090.4 812.3 all-reduce.50
